TPU v7x, 256 devices: a whole 4x4x8 slice. The times are simulated.
256 devices in a mesh: song: 4 (over y), seq: 64 (over z, x, core).
Axes of the slice: x: 4, y: 4, z: 8, core: 2. Of those that a mesh axis runs over, the one named last changes fastest.
Arguments:
- queries: bfloat16 [4, 8192, 2048], P('song', 'seq'), may hold values from -64 to 64
- keys: bfloat16 [4, 8192, 2048], P('song', 'seq'), may hold values from -64 to 64
- values: bfloat16 [4, 8192, 2048], P('song', 'seq'), may hold values from -6 to 6
- lyric_keys: bfloat16 [4, 384, 2048], P('song', 'seq'), may hold values from -64 to 64
- lyric_values: bfloat16 [4, 384, 2048], P('song', 'seq'), may hold values from -6 to 6
- q_gain: float32 [128], replicated, may hold values from 0.5 to 1.5
- k_gain: float32 [128], replicated, may hold values from 0.5 to 1.5
- cotangent: bfloat16 [4, 8192, 2048], P('song', 'seq'), may hold values from -12 to 12
- alignment: int32 [4, 64, 2], P('song', 'seq'), may hold values from -1 to 2, as said below
- lyric_len: int32 [4], P('song'), may hold values from 192 to 384
Outputs:
- attn_out: bfloat16 [4, 8192, 2048], P('song', 'seq')
- grad_queries: bfloat16 [4, 8192, 2048], P('song', 'seq')
- grad_keys: bfloat16 [4, 8192, 2048], P('song', 'seq')
- grad_values: bfloat16 [4, 8192, 2048], P('song', 'seq')
- grad_lyric_keys: bfloat16 [4, 384, 2048], P('song', 'seq')
- grad_lyric_values: bfloat16 [4, 384, 2048], P('song', 'seq')
- grad_q_gain: float32 [128], replicated
- grad_k_gain: float32 [128], replicated
Inputs may be any that keep to these rules, and one draw needn't show every extreme that they name: `alignment`: in each row the entries that are not -1 are distinct.
All inputs are finite; a program needn't handle non-finite values.
Results may differ from a plain program's by a relative error of at most 0.01.
Values may be sent and summed in bfloat16 or wider, within the bound.
A program may use at most 128 MiB of HBM per device.

v0:
```python
import jax
import jax.numpy as jnp
from jax import lax
from jax.sharding import PartitionSpec as P

BLK = 128
WIN = 1
TILES = 2
NORM_EPS = 1e-06


def extended_2(block, sides, width):
    for axis, dim in sides:
        count = lax.axis_size(axis)
        forward = [(i, i + 1) for i in range(count - 1)]
        backward = [(target, source) for source, target in forward]
        low = lax.ppermute(
            lax.slice_in_dim(block, block.shape[dim] - width, None, axis=dim), axis, forward
        )
        high = lax.ppermute(lax.slice_in_dim(block, 0, width, axis=dim), axis, backward)
        block = jnp.concatenate([low, block, high], axis=dim)
    return block


def norm_heads(inputs, norm_gain):
    row_values = inputs.astype(jnp.float32).reshape(inputs.shape[0], -1, norm_gain.shape[0])
    inverse = lax.rsqrt(jnp.mean(row_values * row_values, axis=-1, keepdims=True) + NORM_EPS)
    return (row_values * inverse * norm_gain, inverse)


def norm_back(inputs, inverse, norm_gain, grad_out):
    row_values = inputs.astype(jnp.float32).reshape(grad_out.shape)
    scaled = grad_out * norm_gain
    grad_input = inverse * scaled - row_values * inverse * inverse * inverse * jnp.mean(
        scaled * row_values, axis=-1, keepdims=True
    )
    grad_gain = jnp.sum(grad_out * row_values * inverse, axis=(0, 1))
    return (grad_input.reshape(inputs.shape), grad_gain)


def block_pass(query_rows, key_rows, value_rows, keep_mask, grad_rows, score_scale):
    scores = (
        jnp.einsum("qhd,khd->hqk", query_rows, key_rows, preferred_element_type=jnp.float32)
        * score_scale
    )
    exp_scores = jnp.where(keep_mask[None, None, :], jnp.exp(scores), 0.0)
    totals = jnp.sum(exp_scores, axis=2)
    prob_full = exp_scores / totals[:, :, None]
    prob_low = prob_full.astype(jnp.bfloat16)
    block_output = jnp.einsum(
        "hqk,khd->qhd", prob_low, value_rows, preferred_element_type=jnp.float32
    ).astype(jnp.bfloat16)
    delta_rows = jnp.sum(grad_rows.astype(jnp.float32) * block_output.astype(jnp.float32), axis=2).T
    grad_prob = jnp.einsum(
        "qhd,khd->hqk", grad_rows, value_rows, preferred_element_type=jnp.float32
    )
    grad_score = (prob_full * (grad_prob - delta_rows[:, :, None])).astype(jnp.bfloat16)
    query_gradient = (
        jnp.einsum("hqk,khd->qhd", grad_score, key_rows, preferred_element_type=jnp.float32)
        * score_scale
    )
    grad_key = (
        jnp.einsum("hqk,qhd->khd", grad_score, query_rows, preferred_element_type=jnp.float32)
        * score_scale
    )
    value_gradient = jnp.einsum(
        "hqk,qhd->khd", prob_low, grad_rows, preferred_element_type=jnp.float32
    )
    return (block_output, query_gradient, grad_key, value_gradient, totals, delta_rows)


def body(
    queries, keys, values, lyric_keys, lyric_values, q_gain, k_gain, cotangent, alignment, lyric_len
):
    head_size = q_gain.shape[0]
    model_width = queries.shape[2]
    head_count = model_width // head_size
    frames = queries.shape[1]
    lyric_local = lyric_keys.shape[1]
    blocks = frames // BLK
    border_rows = WIN * BLK
    window_extent = (2 * WIN + 1) * BLK
    score_scale = head_size ** (-0.5)
    total_frames = frames * lax.axis_size("seq")
    first_frame = lax.axis_index("seq") * frames
    query_raw = queries[0]
    key_raw = keys[0]
    query_full, query_inv = norm_heads(query_raw, q_gain)
    key_full, key_inv = norm_heads(key_raw, k_gain)
    lyric_full, lyric_inv = norm_heads(lyric_keys[0], k_gain)
    query_norm = query_full.astype(jnp.bfloat16)
    key_norm = key_full.astype(jnp.bfloat16)
    lyric_norm = lyric_full.astype(jnp.bfloat16)
    lyric_key_all, lyric_val_all = (
        lax.all_gather(lyric_norm.reshape(lyric_local, model_width), "seq", axis=0, tiled=True),
        lax.all_gather(lyric_values[0], "seq", axis=0, tiled=True),
    )
    lyric_total = lyric_key_all.shape[0]
    lyric_key_all = lyric_key_all.reshape(lyric_total, head_count, head_size)
    lyric_val_all = lyric_val_all.reshape(lyric_total, head_count, head_size)
    stacked = jnp.stack([key_norm.reshape(frames, model_width), values[0]])
    extended = extended_2(stacked, (("seq", 1),), border_rows)
    ext_keys = extended[0].reshape(frames + 2 * border_rows, head_count, head_size)
    ext_vals = extended[1].reshape(frames + 2 * border_rows, head_count, head_size)
    grad_heads = cotangent[0].reshape(frames, head_count, head_size)
    length = lyric_len[0]

    def one_block(block_id):
        start_offset = block_id * BLK
        position = (
            first_frame + start_offset - border_rows + jnp.arange(window_extent, dtype=jnp.int32)
        )
        audio_mask = (position >= 0) & (position < total_frames)
        tile_ids = alignment[0, block_id]
        row_grid = (jnp.maximum(tile_ids, 0) * BLK)[:, None] + jnp.arange(BLK, dtype=jnp.int32)[
            None, :
        ]
        lyric_mask = ((tile_ids >= 0)[:, None] & (row_grid < length)).reshape(-1)
        row_index = row_grid.reshape(-1)
        all_keys = jnp.concatenate([ext_keys, jnp.take(lyric_key_all, row_index, axis=0)], axis=0)
        all_vals = jnp.concatenate([ext_vals, jnp.take(lyric_val_all, row_index, axis=0)], axis=0)
        keep_mask = jnp.concatenate([audio_mask, lyric_mask], axis=0)
        results = block_pass(query_norm, all_keys, all_vals, keep_mask, grad_heads, score_scale)
        return results + (row_index,)

    output_list, grad_qn, grad_key, value_gradient, totals, delta_rows, row_index = lax.map(
        one_block, jnp.arange(blocks, dtype=jnp.int32)
    )
    audio_cols = grad_key.shape[1] - TILES * BLK
    flat_rows = row_index.reshape(-1)
    lyric_grad_key = (
        jnp.zeros((lyric_total, head_count, head_size), jnp.float32)
        .at[flat_rows]
        .add(grad_key[:, audio_cols:].reshape(-1, head_count, head_size))
    )
    lyric_grad_val = (
        jnp.zeros((lyric_total, head_count, head_size), jnp.float32)
        .at[flat_rows]
        .add(value_gradient[:, audio_cols:].reshape(-1, head_count, head_size))
    )
    ext_grad_key = jnp.zeros((frames + 2 * border_rows, head_count, head_size), jnp.float32)
    ext_grad_val = jnp.zeros((frames + 2 * border_rows, head_count, head_size), jnp.float32)
    block_id = 0
    lower = block_id * BLK
    ext_grad_key = ext_grad_key.at[lower : lower + window_extent].add(
        grad_key[block_id, :window_extent]
    )
    ext_grad_val = ext_grad_val.at[lower : lower + window_extent].add(
        value_gradient[block_id, :window_extent]
    )
    own_grad_key = ext_grad_key[border_rows : border_rows + frames]
    own_grad_val = ext_grad_val[border_rows : border_rows + frames]
    rims = jnp.stack(
        [
            jnp.concatenate(
                [ext_grad_key[:border_rows], ext_grad_key[border_rows + frames :]], axis=0
            ).reshape(2 * border_rows, model_width),
            jnp.concatenate(
                [ext_grad_val[:border_rows], ext_grad_val[border_rows + frames :]], axis=0
            ).reshape(2 * border_rows, model_width),
        ]
    )
    received = extended_2(rims.astype(jnp.bfloat16), (("seq", 1),), border_rows).astype(rims.dtype)
    from_left = received[:, :border_rows].reshape(2, border_rows, head_count, head_size)
    from_right = received[:, 3 * border_rows :].reshape(2, border_rows, head_count, head_size)
    own_grad_key = (
        own_grad_key.at[:border_rows]
        .add(from_left[0])
        .at[frames - border_rows :]
        .add(from_right[0])
    )
    own_grad_val = (
        own_grad_val.at[:border_rows]
        .add(from_left[1])
        .at[frames - border_rows :]
        .add(from_right[1])
    )
    unnormed_query_gradient, query_gain_vector = norm_back(
        query_raw, query_inv, q_gain, grad_qn.reshape(frames, head_count, head_size)
    )
    unnormed_key_gradient, key_gain_vector = norm_back(key_raw, key_inv, k_gain, own_grad_key)
    summed_key, summed_val = (
        lax.psum_scatter(
            lyric_grad_key.reshape(lyric_total, model_width), "seq", scatter_dimension=0, tiled=True
        ),
        lax.psum_scatter(
            lyric_grad_val.reshape(lyric_total, model_width), "seq", scatter_dimension=0, tiled=True
        ),
    )
    unnormed_lyric_gradient, lyric_gain_vector = norm_back(
        lyric_keys[0], lyric_inv, k_gain, summed_key.reshape(lyric_local, head_count, head_size)
    )
    total_query_gain, total_key_gain = lax.psum(
        (query_gain_vector, key_gain_vector + lyric_gain_vector), ("song", "seq")
    )
    return (
        output_list.reshape(1, frames, model_width),
        unnormed_query_gradient.astype(jnp.bfloat16)[None],
        unnormed_key_gradient.astype(jnp.bfloat16)[None],
        own_grad_val.reshape(1, frames, model_width).astype(jnp.bfloat16),
        unnormed_lyric_gradient.astype(jnp.bfloat16)[None],
        summed_val.astype(jnp.bfloat16)[None],
        total_query_gain,
        total_key_gain,
    )


def solution(mesh):
    in_specs = (
        P("song", "seq", None),
        P("song", "seq", None),
        P("song", "seq", None),
        P("song", "seq", None),
        P("song", "seq", None),
        P(),
        P(),
        P("song", "seq", None),
        P("song", "seq", None),
        P("song"),
    )
    out_specs = (
        P("song", "seq", None),
        P("song", "seq", None),
        P("song", "seq", None),
        P("song", "seq", None),
        P("song", "seq", None),
        P("song", "seq", None),
        P(),
        P(),
    )
    return jax.shard_map(body, mesh=mesh, in_specs=in_specs, out_specs=out_specs, check_vma=False)
```

profile of v0, /device:TPU:1, one launch (start us, length us, event | category | flops | bytes accessed | tf_op | source)
XLA Modules:
  0.0 654.3 jit_solution(4677205366677550377)
XLA Ops:
  7.2 1.4 copy.99
  8.7 0.8 convert_bitcast_fusion
  9.6 0.7 broadcast_bitcast_fusion.2
  10.3 1.4 fusion.41
  11.8 1.3 copy.98
  13.1 1.4 copy.97
  14.5 1.2 multiply_reduce_fusion.2
  15.7 0.4 multiply_convert_fusion.1
  16.2 5.2 collective-permute-start.1
  21.4 1.9 collective-permute-start
  24.1 1.0 copy.107
  25.1 1.2 copy.103
  26.4 0.7 dynamic-slice.30
  27.9 5.7 collective-permute-done.1
  33.6 1.9 collective-permute-done
  35.5 1.7 pad_maximum_fusion
  37.3 1.5 fusion.52
  38.8 1.6 copy.105
  40.4 53.5 %all-gather.5.cloned.1.call-done = bf16[1,384,2048]{2,0,1:T(2,128)(2,1)} async-done(((bf16[1,6,2048]{2,0,1:T(2,128)(2,1)}), bf16[1,384,2048]{2,0,1:T(2,128)(2,1)}) %all-gather.5.cloned.1.call-update) | async-done | bytes 1572880 | tf_op jit(solution)/shard_map/all_gather | solution.py:96
  93.9 6.9 %copy.100 = bf16[1,384,2048]{1,2,0:T(8,128)(2,1)S(1)} copy(bf16[1,384,2048]{2,0,1:T(2,128)(2,1)} %all-gather.5.cloned.1.call-done) | data formatting | bytes 3145728 | tf_op jit(solution)/shard_map/all_gather | solution.py:96
  100.9 2.0 copy.101
  102.9 69.1 %all-gather.7.cloned.1.call-done = bf16[64,6,2048]{2,1,0:T(8,128)(2,1)} async-done(((bf16[1,6,2048]{2,1,0:T(8,128)(2,1)}), bf16[64,6,2048]{2,1,0:T(8,128)(2,1)}) %all-gather.7.cloned.1.call-update) | async-done | bytes 1572880 | tf_op jit(solution)/shard_map/all_gather | solution.py:95
  172.0 4.4 reshape.472
  176.4 3.2 gather_fusion.1
  179.6 1.8 gather_fusion
  181.3 1.6 copy.102
  183.0 1.6 copy_select_fusion
  184.7 1.6 fusion.2
  186.3 3.1 fusion.56
  189.5 2.4 multiply_reduce_fusion
  191.9 1.8 fusion
  193.7 0.9 fusion.57
  194.6 0.6 copy-done.14
  195.3 0.3 fusion.54
  195.8 0.3 maximum_maximum_fusion
  196.1 0.5 copy-done.5
  196.8 2.1 fusion.55
  198.9 2.1 collective-permute-start.3
  201.0 3.6 collective-permute-start.2
  204.8 2.0 copy.112
  206.8 0.2 broadcast.403.clone
  207.0 20.2 %scatter_fusion = f32[384,16,128]{2,1,0:T(8,128)S(1)} fusion(f32[384,16,128]{2,1,0:T(8,128)S(1)} %broadcast.403.clone, s32[256]{0:T(256)S(1)} %bitcast.227, f32[256,16,128]{2,1,0:T(8,128)} %copy.112), kind=kCustom, calls=%fused_computation.2 | custom fusion | flops 524288 | bytes 6292480 | tf_op jit(solution)/shard_map/scatter-add | solution.py:134
  227.3 3.1 copy.146
  230.3 1.8 slice_bitcast_fusion
  232.1 2.0 copy.113
  234.4 20.2 %scatter_fusion.1 = f32[384,16,128]{2,1,0:T(8,128)S(1)} fusion(f32[384,16,128]{2,1,0:T(8,128)S(1)} %broadcast.403.clone.1, s32[256]{0:T(256)S(1)} %bitcast.228, f32[256,16,128]{2,1,0:T(8,128)} %copy.113), kind=kCustom, calls=%fused_computation.3 | custom fusion | flops 524288 | bytes 6292480 | tf_op jit(solution)/shard_map/scatter-add | solution.py:139
  254.6 3.1 copy.145
  257.7 279.7 %all-reduce.7 = bf16[384,2048]{1,0:T(8,128)(2,1)} all-reduce(f32[384,2048]{1,0:T(8,128)} %bitcast.203), channel_id=4, replica_groups=mesh['song'=4,'seq'=64] {'seq'}, use_global_device_ids=true, to_apply=%region_11.13.clone | all-reduce | flops 786432 | bytes 4718592
  537.4 4.1 fusion.18
  541.6 1.3 slice.221
  542.9 2.4 slice.228
  545.3 2.0 copy.114
  547.4 2.3 fusion.25
  549.7 2.0 copy.115
  551.7 1.5 fusion.40
  553.2 1.8 fusion.14
  555.0 1.6 fusion.22
  556.7 1.2 fusion.12
  557.9 2.0 copy.116
  559.9 1.7 fusion.16
  561.6 1.0 copy.117
  562.7 0.9 dynamic-slice_bitcast_fusion
  563.8 1.6 fusion.33
  565.4 82.4 %all-reduce.2 = (f32[128]{0:T(128)}, f32[128]{0:T(128)}) all-reduce(f32[128]{0:T(128)S(1)} %get-tuple-element.214, f32[128]{0:T(128)S(1)} %add.202), channel_id=1, replica_groups=mesh['song'=4,'seq'=64] {'song','seq'}, use_global_device_ids=true, to_apply=%region_13.15 | all-reduce | flops 256 | bytes 2048 | tf_op jit(solution)/shard_map/psum | solution.py:193
  (86 shorter events, 1.9 us)
Async XLA Ops:
  7.2 86.8 %all-gather.5.cloned.1.call-start = ((), (), s32[]{:S(2)}) async-start(), calls=%async_computation | async-start | bytes 3194880 | tf_op jit(solution)/shard_map/all_gather | solution.py:96
  8.7 163.3 %all-gather.7.cloned.1.call-start = ((), (), s32[]{:S(2)}) async-start(), calls=%async_computation.1 | async-start | bytes 2129920 | tf_op jit(solution)/shard_map/all_gather | solution.py:95
  11.7 550.9 %all-reduce.6.cloned.1.call-start = ((), (), s32[]{:S(2)}) async-start(), calls=%async_computation.2 | async-start | bytes 6291456
  13.1 10.9 %copy-start.24 = (s32[1,1,2]{2,1,0:T(1,128)S(1)}, s32[1,1,2]{2,1,0:T(1,128)}, u32[]{:S(2)}) copy-start(s32[1,1,2]{2,1,0:T(1,128)} %param.44) | copy-start | bytes 28
  13.1 11.0 %copy-start.19 = (bf16[1,128,2048]{2,1,0:T(8,128)(2,1)S(1)}, bf16[1,128,2048]{2,1,0:T(8,128)(2,1)}, u32[]{:S(2)}) copy-start(bf16[1,128,2048]{2,1,0:T(8,128)(2,1)} %param.43) | copy-start | bytes 1572868
  14.5 9.6 %copy-start.3 = (bf16[1,128,2048]{1,2,0:T(8,128)(2,1)}, bf16[1,128,2048]{1,2,0:T(8,128)(2,1)S(1)}, u32[]{:S(2)}) copy-start(bf16[1,128,2048]{1,2,0:T(8,128)(2,1)S(1)} %copy.97) | copy-start | bytes 1572868
  15.7 10.7 %copy-start.25 = (u32[256]{0:T(256)S(1)}, u32[256]{0:T(256)}, u32[]{:S(2)}) copy-start(u32[256]{0:T(256)} %constant.274) | copy-start | bytes 3076
  16.1 11.7 %copy-start.23 = (f32[128]{0:T(128)S(1)}, f32[128]{0:T(128)}, u32[]{:S(2)}) copy-start(f32[128]{0:T(128)} %param.41) | copy-start | bytes 1540
  16.2 17.4 %collective-permute-start.1 = (bf16[2,128,2048]{1,2,0:T(8,128)(2,1)S(1)}, bf16[2,128,2048]{1,2,0:T(8,128)(2,1)}, u32[]{:S(2)}, u32[]{:S(2)}) collective-permute-start(bf16[2,128,2048]{1,2,0:T(8,128)(2,1)S(1)} %pad_maximum_fusion.9), channel_id=1, source_target_pairs={{1,0},{2,1},{3,2},{4,3},{5,4},{6,5},{7,6},{8,7},{9,8},{10,9},{11,1... | collective-permute-start | bytes 3145736 | tf_op jit(solution)/shard_map/ppermute | solution.py:20
  21.4 14.2 %collective-permute-start = (bf16[2,128,2048]{1,2,0:T(8,128)(2,1)S(1)}, bf16[2,128,2048]{1,2,0:T(8,128)(2,1)}, u32[]{:S(2)}, u32[]{:S(2)}) collective-permute-start(bf16[2,128,2048]{1,2,0:T(8,128)(2,1)S(1)} %pad_maximum_fusion.9), channel_id=1, source_target_pairs={{0,1},{1,2},{2,3},{3,4},{4,5},{5,6},{6,7},{7,8},{8,9},{9,10},{10,1... | collective-permute-start | bytes 3145736 | tf_op jit(solution)/shard_map/ppermute | solution.py:17
  26.4 167.4 %copy-start.1 = (f32[1,128,2048]{1,2,0:T(8,128)}, f32[1,128,2048]{1,2,0:T(8,128)S(1)}, u32[]{:S(2)}) copy-start(f32[1,128,2048]{1,2,0:T(8,128)S(1)} %copy.103) | copy-start | bytes 3145732
  102.9 76.7 %copy-start.12 = (bf16[384,16,128]{2,1,0:T(8,128)(2,1)S(1)}, bf16[384,16,128]{2,1,0:T(8,128)(2,1)}, u32[]{:S(2)}) copy-start(bf16[384,16,128]{2,1,0:T(8,128)(2,1)} %copy.101) | copy-start | bytes 4718596
  183.0 1.8 copy-start.15
  184.6 1.7 copy-start.18
  184.7 1.6 copy-start.20
  186.3 3.1 copy-start.17
  193.7 1.5 copy-start.14
  195.3 9.4 %copy-start = (f32[1,640,16,128]{1,3,2,0:T(8,128)}, f32[1,640,16,128]{1,3,2,0:T(8,128)S(1)}, u32[]{:S(2)}) copy-start(f32[1,640,16,128]{1,3,2,0:T(8,128)S(1)} %get-tuple-element.244) | copy-start | bytes 15728644
  195.6 1.0 copy-start.5
  195.6 1.2 copy-start.7
  195.8 3.1 copy-start.9
  195.8 3.1 copy-start.11
  198.9 354.3 %collective-permute-start.3 = (bf16[2,128,2048]{1,2,0:T(8,128)(2,1)}, bf16[2,128,2048]{1,2,0:T(8,128)(2,1)}, u32[]{:S(2)}, u32[]{:S(2)}) collective-permute-start(bf16[2,128,2048]{1,2,0:T(8,128)(2,1)} %get-tuple-element.234), channel_id=1, source_target_pairs={{1,0},{2,1},{3,2},{4,3},{5,4},{6,5},{7,6},{8,7},{9,8},{10,9},{11,1... | collective-permute-start | bytes 3145736 | tf_op jit(solution)/shard_map/ppermute | solution.py:20
  201.0 352.2 %collective-permute-start.2 = (bf16[2,128,2048]{1,2,0:T(8,128)(2,1)}, bf16[2,128,2048]{1,2,0:T(8,128)(2,1)}, u32[]{:S(2)}, u32[]{:S(2)}) collective-permute-start(bf16[2,128,2048]{1,2,0:T(8,128)(2,1)} %get-tuple-element.233), channel_id=1, source_target_pairs={{0,1},{1,2},{2,3},{3,4},{4,5},{5,6},{6,7},{7,8},{8,9},{9,10},{10,1... | collective-permute-start | bytes 3145736 | tf_op jit(solution)/shard_map/ppermute | solution.py:17
  257.7 279.7 %copy-start.2 = (f32[1,128,2048]{1,2,0:T(8,128)S(1)}, f32[1,128,2048]{1,2,0:T(8,128)}, u32[]{:S(2)}) copy-start(f32[1,128,2048]{1,2,0:T(8,128)} %copy-done.1) | copy-start | bytes 3145732
  257.7 279.7 %copy-start.16 = (bf16[384,16,128]{2,0,1:T(8,128)(2,1)S(1)}, bf16[384,16,128]{2,0,1:T(8,128)(2,1)}, u32[]{:S(2)}) copy-start(bf16[384,16,128]{2,0,1:T(8,128)(2,1)} %copy.105) | copy-start | bytes 4718596
  542.9 10.3 %copy-start.4 = (bf16[1,128,2048]{1,2,0:T(8,128)(2,1)S(1)}, bf16[1,128,2048]{1,2,0:T(8,128)(2,1)}, u32[]{:S(2)}) copy-start(bf16[1,128,2048]{1,2,0:T(8,128)(2,1)} %copy-done.3) | copy-start | bytes 1572868
  542.9 10.3 %copy-start.6 = (bf16[1,128,16,128]{1,3,2,0:T(8,128)(2,1)S(1)}, bf16[1,128,16,128]{1,3,2,0:T(8,128)(2,1)}, u32[]{:S(2)}) copy-start(bf16[1,128,16,128]{1,3,2,0:T(8,128)(2,1)} %copy-done.5) | copy-start | bytes 1572868
  553.2 1.8 copy-start.13
  553.2 1.8 copy-start.22
  556.6 3.3 copy-start.8
  556.6 3.3 copy-start.10
  559.9 3.8 copy-start.21
Sparse Core Ops, SparseCore 0:
  11.3 82.5 all-gather.4
  97.3 74.6 all-gather.6
  230.5 192.0 all-reduce.5
where the time goes:
time: 656 us; the launch traced here: 654 us
  blocking collectives  362 us (55%)
  waiting for transfers between devices  130 us (20%)
  local copies, waits for them, and re-layouts  60.6 us (9%)
  other arithmetic  58.7 us (9%)
  between operations  15.6 us (2%)
  matrix products  14 us (2%)
  starting transfers between devices  12.9 us (2%)
    unnamed x1, blocking collectives  280 us
    psum x1, blocking collectives, body(): lax.psum((query_gain_vector, key_gain_vector + lyric_gain_vector), ('song...  82.4 us
    all_gather x1, waiting for transfers between devices, body(): lax.all_gather(lyric_norm.reshape(lyric_local, model_width), 'seq', axis=...  69.1 us
    all_gather x1, waiting for transfers between devices, body(): lax.all_gather(lyric_values[0], 'seq', axis=0, tiled=True)  53.5 us
    unnamed x66, local copies, waits for them, and re-layouts  21.5 us
    scatter-add x1, other arithmetic, body(): lyric_grad_val = jnp.zeros((lyric_total, head_count, head_size), jnp.floa...  20.2 us
    scatter-add x1, other arithmetic, body(): lyric_grad_key = jnp.zeros((lyric_total, head_count, head_size), jnp.floa...  20.2 us
  transfers between devices with their start and end apart: 7, of which 4 were waited for; matrix products, arithmetic and copies ran while one was open for 16% of the time, Pallas kernels for 0%

commit v1 on v0

--- a/solution.py
+++ b/solution.py
@@ -7,6 +7,11 @@
 WIN = 1
 TILES = 2
 NORM_EPS = 1e-06
+
+
+def gather_over(block, axis, along):
+    stack = jnp.stack([block] * lax.axis_size(axis))
+    return jnp.concatenate(lax.all_to_all(stack, axis, 0, 0), axis=along)
 
 
 def extended_2(block, sides, width):
@@ -93,7 +98,7 @@
     lyric_norm = lyric_full.astype(jnp.bfloat16)
     lyric_key_all, lyric_val_all = (
         lax.all_gather(lyric_norm.reshape(lyric_local, model_width), "seq", axis=0, tiled=True),
-        lax.all_gather(lyric_values[0], "seq", axis=0, tiled=True),
+        gather_over(lyric_values[0], "seq", 0),
     )
     lyric_total = lyric_key_all.shape[0]
     lyric_key_all = lyric_key_all.reshape(lyric_total, head_count, head_size)

time: 656 us -> 588 us (0.90)
  waiting for transfers between devices: 130 us -> 47.2 us
  starting transfers between devices: 12.9 us -> 24.6 us
    all_gather x1 -> x0, waiting for transfers between devices: 53.5 us -> none  [body(): lax.all_gather(lyric_values[0], 'seq', axis=0, tiled=True)]
    all_gather x1, waiting for transfers between devices: 69.1 us -> 32.4 us  [body(): lax.all_gather(lyric_norm.reshape(lyric_local, model_width), 'seq', axis=...]
    all_to_all x0 -> x1, starting transfers between devices: none -> 13 us  [gather_over(): return jnp.concatenate(lax.all_to_all(stack, axis, 0, 0), axis=along)]
    ppermute x2, waiting for transfers between devices: 5.67 us -> 14.2 us  [extended_2(): lax.ppermute(lax.slice_in_dim(block, 0, width, axis=dim), axis, backward)]
    all_gather x1 -> x0, local copies, waits for them, and re-layouts: 6.94 us -> none  [body(): lax.all_gather(lyric_values[0], 'seq', axis=0, tiled=True)]
    unnamed x66 -> x69, local copies, waits for them, and re-layouts: 21.5 us -> 22.4 us
  transfers between devices with their start and end apart: 7 -> 7, of which waited for: 4 -> 3; matrix products, arithmetic and copies ran while one was open for 16% -> 18% of each run, Pallas kernels for 0% -> 0%
where the time goes in v1:
time: 588 us; the launch traced here: 586 us
  blocking collectives  365 us (62%)
  local copies, waits for them, and re-layouts  60.5 us (10%)
  other arithmetic  58.7 us (10%)
  waiting for transfers between devices  47.2 us (8%)
  starting transfers between devices  24.6 us (4%)
  between operations  15.9 us (3%)
  matrix products  14 us (2%)
    unnamed x1, blocking collectives  279 us
    psum x1, blocking collectives, body(): lax.psum((query_gain_vector, key_gain_vector + lyric_gain_vector), ('song...  85.7 us
    all_gather x1, waiting for transfers between devices, body(): lax.all_gather(lyric_norm.reshape(lyric_local, model_width), 'seq', axis=...  32.4 us
    unnamed x69, local copies, waits for them, and re-layouts  22.4 us
    scatter-add x1, other arithmetic, body(): lyric_grad_val = jnp.zeros((lyric_total, head_count, head_size), jnp.floa...  20.2 us
    scatter-add x1, other arithmetic, body(): lyric_grad_key = jnp.zeros((lyric_total, head_count, head_size), jnp.floa...  20.2 us
    ppermute x2, waiting for transfers between devices, extended_2(): lax.ppermute(lax.slice_in_dim(block, 0, width, axis=dim), axis, backward)  14.2 us
    all_to_all x1, starting transfers between devices, gather_over(): return jnp.concatenate(lax.all_to_all(stack, axis, 0, 0), axis=along)  13 us
  transfers between devices with their start and end apart: 7, of which 3 were waited for; matrix products, arithmetic and copies ran while one was open for 18% of the time, Pallas kernels for 0%

profile of v1, /device:TPU:1, one launch (start us, length us, event | category | flops | bytes accessed | tf_op | source)
XLA Modules:
  0.0 586.0 jit_solution(6345696655939693160)
XLA Ops:
  7.2 0.8 convert_bitcast_fusion
  8.1 0.7 broadcast_bitcast_fusion.2
  8.8 1.4 fusion.41
  10.3 2.4 stack.11
  12.7 13.0 %all-to-all-start = ((bf16[64,6,2048]{2,1,0:T(8,128)(2,1)}), bf16[64,6,2048]{2,1,0:T(8,128)(2,1)S(1)}, u32[]{:S(2)}, u32[]{:S(2)}) async-start(bf16[64,6,2048]{2,1,0:T(8,128)(2,1)} %stack.11), calls=%async_computation | async-start | bytes 4194304 | tf_op jit(solution)/shard_map/all_to_all | solution.py:14
  25.7 0.3 copy.76
  26.0 1.5 copy.75
  27.5 1.2 multiply_reduce_fusion.2
  28.8 0.4 multiply_convert_fusion.1
  29.2 0.8 copy-done.13
  30.0 1.1 pad_maximum_fusion.9
  31.0 2.4 collective-permute-start.1
  33.4 3.4 collective-permute-start
  37.6 2.0 copy.82
  39.6 1.2 copy.78
  40.9 0.7 dynamic-slice.30
  42.4 14.2 %collective-permute-done.1 = bf16[2,128,2048]{1,2,0:T(8,128)(2,1)} collective-permute-done((bf16[2,128,2048]{1,2,0:T(8,128)(2,1)}, bf16[2,128,2048]{1,2,0:T(8,128)(2,1)}, u32[]{:S(2)}, u32[]{:S(2)}) %collective-permute-start.1) | collective-permute-done | bytes 1048608 | tf_op jit(solution)/shard_map/ppermute | solution.py:25
  56.6 0.6 collective-permute-done
  57.2 2.1 pad_maximum_fusion
  59.3 1.9 fusion.52
  61.2 2.6 copy.80
  63.8 32.4 %all-gather.3.cloned.1.call-done = bf16[64,6,2048]{2,1,0:T(8,128)(2,1)} async-done(((bf16[1,6,2048]{2,1,0:T(8,128)(2,1)}), bf16[64,6,2048]{2,1,0:T(8,128)(2,1)}) %all-gather.3.cloned.1.call-update) | async-done | bytes 1572880 | tf_op jit(solution)/shard_map/all_gather | solution.py:100
  96.3 4.4 reshape.469
  100.6 3.2 gather_fusion.1
  103.8 2.7 reshape_reshape.3
  106.5 3.3 gather_fusion
  109.7 1.6 copy.77
  111.8 1.4 copy-done.17
  113.2 1.5 fusion.2
  114.7 3.1 fusion.56
  117.9 2.4 multiply_reduce_fusion
  120.3 1.8 fusion
  122.2 0.9 fusion.57
  123.1 0.6 copy-done.16
  123.7 0.3 fusion.54
  124.2 0.3 maximum_maximum_fusion
  124.5 0.5 copy-done.5
  125.2 2.1 fusion.55
  127.3 2.1 collective-permute-start.3
  129.4 3.6 collective-permute-start.2
  133.3 2.0 copy.87
  135.4 20.2 %scatter_fusion = f32[384,16,128]{2,1,0:T(8,128)S(1)} fusion(f32[384,16,128]{2,1,0:T(8,128)S(1)} %broadcast.404.clone, s32[256]{0:T(256)S(1)} %bitcast.227, f32[256,16,128]{2,1,0:T(8,128)} %copy.87), kind=kCustom, calls=%fused_computation.2 | custom fusion | flops 524288 | bytes 6292480 | tf_op jit(solution)/shard_map/scatter-add | solution.py:139
  155.7 3.0 copy.121
  158.7 1.8 slice_bitcast_fusion
  160.5 2.0 copy.88
  162.8 20.2 %scatter_fusion.1 = f32[384,16,128]{2,1,0:T(8,128)S(1)} fusion(f32[384,16,128]{2,1,0:T(8,128)S(1)} %broadcast.404.clone.1, s32[256]{0:T(256)S(1)} %bitcast.228, f32[256,16,128]{2,1,0:T(8,128)} %copy.88), kind=kCustom, calls=%fused_computation.3 | custom fusion | flops 524288 | bytes 6292480 | tf_op jit(solution)/shard_map/scatter-add | solution.py:144
  183.0 3.1 copy.120
  186.1 279.4 %all-reduce.7 = bf16[384,2048]{1,0:T(8,128)(2,1)} all-reduce(f32[384,2048]{1,0:T(8,128)} %bitcast.203), channel_id=3, replica_groups=mesh['song'=4,'seq'=64] {'seq'}, use_global_device_ids=true, to_apply=%region_11.13.clone | all-reduce | flops 786432 | bytes 4718592
  465.5 4.2 fusion.18
  469.7 1.3 slice.221
  471.0 2.4 slice.228
  473.4 2.0 copy.89
  475.5 2.3 fusion.25
  477.8 2.0 copy.90
  479.8 1.5 fusion.40
  481.3 1.8 fusion.14
  483.1 1.6 fusion.22
  484.8 1.2 fusion.12
  486.0 2.0 copy.91
  488.1 1.7 fusion.16
  489.8 1.0 copy.92
  490.8 0.9 dynamic-slice_bitcast_fusion
  491.9 1.6 fusion.33
  493.5 85.7 %all-reduce.2 = (f32[128]{0:T(128)}, f32[128]{0:T(128)}) all-reduce(f32[128]{0:T(128)S(1)} %get-tuple-element.206, f32[128]{0:T(128)S(1)} %add.202), channel_id=1, replica_groups=mesh['song'=4,'seq'=64] {'song','seq'}, use_global_device_ids=true, to_apply=%region_13.15 | all-reduce | flops 256 | bytes 2048 | tf_op jit(solution)/shard_map/psum | solution.py:198
  (88 shorter events, 2.2 us)
Async XLA Ops:
  7.2 89.1 %all-gather.3.cloned.1.call-start = ((), (), s32[]{:S(2)}) async-start(), calls=%async_computation.1 | async-start | bytes 2129920 | tf_op jit(solution)/shard_map/all_gather | solution.py:100
  10.2 15.5 %copy-start.21 = (bf16[1,128,2048]{2,1,0:T(8,128)(2,1)S(1)}, bf16[1,128,2048]{2,1,0:T(8,128)(2,1)}, u32[]{:S(2)}) copy-start(bf16[1,128,2048]{2,1,0:T(8,128)(2,1)} %param.38) | copy-start | bytes 1572868
  12.7 91.1 %all-to-all-start = ((bf16[64,6,2048]{2,1,0:T(8,128)(2,1)}), bf16[64,6,2048]{2,1,0:T(8,128)(2,1)S(1)}, u32[]{:S(2)}, u32[]{:S(2)}) async-start(bf16[64,6,2048]{2,1,0:T(8,128)(2,1)} %stack.11), calls=%async_computation | async-start | bytes 4194304 | tf_op jit(solution)/shard_map/all_to_all | solution.py:14
  25.7 465.1 %all-reduce.6.cloned.1.call-start = ((), (), s32[]{:S(2)}) async-start(), calls=%async_computation.2 | async-start | bytes 6291456
  26.0 11.6 %copy-start.12 = (bf16[1,128,2048]{1,2,0:T(8,128)(2,1)}, bf16[1,128,2048]{1,2,0:T(8,128)(2,1)S(1)}, u32[]{:S(2)}) copy-start(bf16[1,128,2048]{1,2,0:T(8,128)(2,1)S(1)} %copy.76) | copy-start | bytes 1572868
  26.0 11.4 %copy-start.26 = (s32[1,1,2]{2,1,0:T(1,128)S(1)}, s32[1,1,2]{2,1,0:T(1,128)}, u32[]{:S(2)}) copy-start(s32[1,1,2]{2,1,0:T(1,128)} %param.44) | copy-start | bytes 28
  27.5 10.0 %copy-start.3 = (bf16[1,128,2048]{1,2,0:T(8,128)(2,1)}, bf16[1,128,2048]{1,2,0:T(8,128)(2,1)S(1)}, u32[]{:S(2)}) copy-start(bf16[1,128,2048]{1,2,0:T(8,128)(2,1)S(1)} %copy.75) | copy-start | bytes 1572868
  28.8 12.1 %copy-start.27 = (u32[256]{0:T(256)S(1)}, u32[256]{0:T(256)}, u32[]{:S(2)}) copy-start(u32[256]{0:T(256)} %constant.274) | copy-start | bytes 3076
  29.2 0.8 copy-start.13
  30.0 12.4 %copy-start.25 = (f32[128]{0:T(128)S(1)}, f32[128]{0:T(128)}, u32[]{:S(2)}) copy-start(f32[128]{0:T(128)} %param.41) | copy-start | bytes 1540
  31.0 25.6 %collective-permute-start.1 = (bf16[2,128,2048]{1,2,0:T(8,128)(2,1)}, bf16[2,128,2048]{1,2,0:T(8,128)(2,1)}, u32[]{:S(2)}, u32[]{:S(2)}) collective-permute-start(bf16[2,128,2048]{1,2,0:T(8,128)(2,1)} %pad_maximum_fusion.9), channel_id=1, source_target_pairs={{1,0},{2,1},{3,2},{4,3},{5,4},{6,5},{7,6},{8,7},{9,8},{10,9},{11,1... | collective-permute-start | bytes 3145736 | tf_op jit(solution)/shard_map/ppermute | solution.py:25
  33.4 23.9 %collective-permute-start = (bf16[2,128,2048]{1,2,0:T(8,128)(2,1)}, bf16[2,128,2048]{1,2,0:T(8,128)(2,1)}, u32[]{:S(2)}, u32[]{:S(2)}) collective-permute-start(bf16[2,128,2048]{1,2,0:T(8,128)(2,1)} %pad_maximum_fusion.9), channel_id=1, source_target_pairs={{0,1},{1,2},{2,3},{3,4},{4,5},{5,6},{6,7},{7,8},{8,9},{9,10},{10,1... | collective-permute-start | bytes 3145736 | tf_op jit(solution)/shard_map/ppermute | solution.py:22
  40.9 81.3 %copy-start.1 = (f32[1,128,2048]{1,2,0:T(8,128)}, f32[1,128,2048]{1,2,0:T(8,128)S(1)}, u32[]{:S(2)}) copy-start(f32[1,128,2048]{1,2,0:T(8,128)S(1)} %copy.78) | copy-start | bytes 3145732
  106.5 4.9 copy-start.15
  111.4 1.8 copy-start.17
  111.7 3.1 copy-start.20
  113.2 1.6 copy-start.22
  114.7 3.1 copy-start.19
  122.1 1.5 copy-start.16
  123.7 9.4 %copy-start = (f32[1,640,16,128]{1,3,2,0:T(8,128)}, f32[1,640,16,128]{1,3,2,0:T(8,128)S(1)}, u32[]{:S(2)}) copy-start(f32[1,640,16,128]{1,3,2,0:T(8,128)S(1)} %get-tuple-element.236) | copy-start | bytes 15728644
  124.0 1.0 copy-start.5
  124.0 1.2 copy-start.7
  124.2 3.1 copy-start.9
  124.2 3.1 copy-start.11
  127.3 354.0 %collective-permute-start.3 = (bf16[2,128,2048]{1,2,0:T(8,128)(2,1)}, bf16[2,128,2048]{1,2,0:T(8,128)(2,1)}, u32[]{:S(2)}, u32[]{:S(2)}) collective-permute-start(bf16[2,128,2048]{1,2,0:T(8,128)(2,1)} %get-tuple-element.226), channel_id=1, source_target_pairs={{1,0},{2,1},{3,2},{4,3},{5,4},{6,5},{7,6},{8,7},{9,8},{10,9},{11,1... | collective-permute-start | bytes 3145736 | tf_op jit(solution)/shard_map/ppermute | solution.py:25
  129.4 351.9 %collective-permute-start.2 = (bf16[2,128,2048]{1,2,0:T(8,128)(2,1)}, bf16[2,128,2048]{1,2,0:T(8,128)(2,1)}, u32[]{:S(2)}, u32[]{:S(2)}) collective-permute-start(bf16[2,128,2048]{1,2,0:T(8,128)(2,1)} %get-tuple-element.225), channel_id=1, source_target_pairs={{0,1},{1,2},{2,3},{3,4},{4,5},{5,6},{6,7},{7,8},{8,9},{9,10},{10,1... | collective-permute-start | bytes 3145736 | tf_op jit(solution)/shard_map/ppermute | solution.py:22
  186.1 279.4 %copy-start.2 = (f32[1,128,2048]{1,2,0:T(8,128)S(1)}, f32[1,128,2048]{1,2,0:T(8,128)}, u32[]{:S(2)}) copy-start(f32[1,128,2048]{1,2,0:T(8,128)} %copy-done.1) | copy-start | bytes 3145732
  186.1 279.4 %copy-start.18 = (bf16[384,16,128]{2,0,1:T(8,128)(2,1)S(1)}, bf16[384,16,128]{2,0,1:T(8,128)(2,1)}, u32[]{:S(2)}) copy-start(bf16[384,16,128]{2,0,1:T(8,128)(2,1)} %copy.80) | copy-start | bytes 4718596
  471.0 10.3 %copy-start.4 = (bf16[1,128,2048]{1,2,0:T(8,128)(2,1)S(1)}, bf16[1,128,2048]{1,2,0:T(8,128)(2,1)}, u32[]{:S(2)}) copy-start(bf16[1,128,2048]{1,2,0:T(8,128)(2,1)} %copy-done.3) | copy-start | bytes 1572868
  471.0 10.3 %copy-start.6 = (bf16[1,128,16,128]{1,3,2,0:T(8,128)(2,1)S(1)}, bf16[1,128,16,128]{1,3,2,0:T(8,128)(2,1)}, u32[]{:S(2)}) copy-start(bf16[1,128,16,128]{1,3,2,0:T(8,128)(2,1)} %copy-done.5) | copy-start | bytes 1572868
  481.3 1.8 copy-start.14
  481.3 1.8 copy-start.24
  484.7 3.3 copy-start.8
  484.8 3.3 copy-start.10
  488.1 3.8 copy-start.23
Sparse Core Ops, SparseCore 0:
  11.3 84.8 all-gather.2
  158.9 194.5 all-reduce.5
